TPU v7x, 32 devices: a whole 2x2x4 slice. The times are simulated.
32 devices in a mesh: items: 4 (over x, core), rows: 8 (over z, y).
Axes of the slice: x: 2, y: 2, z: 4, core: 2. Of those that a mesh axis runs over, the one named last changes fastest.
Arguments:
- tokens: bfloat16 [16384, 768], P(('items', 'rows')), may hold values from -6 to 6
- query_proj: bfloat16 [768, 768], P(('items', 'rows')), may hold values from -0.21875 to 0.21875
- key_proj: bfloat16 [768, 768], P(('items', 'rows')), may hold values from -0.21875 to 0.21875
- value_proj: bfloat16 [768, 768], P(('items', 'rows')), may hold values from -0.21875 to 0.21875
- query_bias: bfloat16 [768], P(('items', 'rows')), may hold values from -1.5 to 1.5
- value_bias: bfloat16 [768], P(('items', 'rows')), may hold values from -0.25 to 0.25
- output_proj: bfloat16 [768, 768], P(('items', 'rows')), may hold values from -0.875 to 0.875
- output_bias: bfloat16 [768], P(('items', 'rows')), may hold values from -1 to 1
- attn_gain: bfloat16 [768], P(('items', 'rows')), may hold values from 0.099609375 to 1.8984375
- attn_shift: bfloat16 [768], P(('items', 'rows')), may hold values from -1 to 1
- hidden_proj: bfloat16 [768, 3072], P(('items', 'rows')), may hold values from -0.21875 to 0.21875
- hidden_bias: bfloat16 [3072], P(('items', 'rows')), may hold values from -1 to 1
- return_proj: bfloat16 [3072, 768], P(('items', 'rows')), may hold values from -0.109375 to 0.109375
- return_bias: bfloat16 [768], P(('items', 'rows')), may hold values from -1 to 1
- final_gain: bfloat16 [768], P(('items', 'rows')), may hold values from 0.099609375 to 1.8984375
- final_shift: bfloat16 [768], P(('items', 'rows')), may hold values from -2.5 to 2.5
- item_lengths: int32 [4, 8], P('items'), may hold values from 1 to 1024, 4096 in all within a row
- out_grad: bfloat16 [16384, 768], P(('items', 'rows')), may hold values from -6 to 6
Outputs:
- layer_out: bfloat16 [16384, 768], P(('items', 'rows'))
- tokens_grad: float32 [16384, 768], P(('items', 'rows'))
- grad_query_proj: float32 [768, 768], P(('items', 'rows'))
- grad_key_proj: float32 [768, 768], P(('items', 'rows'))
- grad_value_proj: float32 [768, 768], P(('items', 'rows'))
- grad_query_bias: float32 [768], P(('items', 'rows'))
- grad_value_bias: float32 [768], P(('items', 'rows'))
- grad_output_proj: float32 [768, 768], P(('items', 'rows'))
- grad_output_bias: float32 [768], P(('items', 'rows'))
- grad_attn_gain: float32 [768], P(('items', 'rows'))
- grad_attn_shift: float32 [768], P(('items', 'rows'))
- grad_hidden_proj: float32 [768, 3072], P(('items', 'rows'))
- grad_hidden_bias: float32 [3072], P(('items', 'rows'))
- grad_return_proj: float32 [3072, 768], P(('items', 'rows'))
- grad_return_bias: float32 [768], P(('items', 'rows'))
- grad_final_gain: float32 [768], P(('items', 'rows'))
- grad_final_shift: float32 [768], P(('items', 'rows'))
Inputs may be any that keep to these rules, and one draw needn't show every extreme that they name: `item_lengths`: each row lists the lengths of its group's 8 items in stream order and sums to 4096; in each row one item has exactly 1024 tokens.
All inputs are finite; a program needn't handle non-finite values.
Results may differ from a plain program's by a relative error of at most 0.014.
Values may be sent and summed in bfloat16 or wider, within the bound.
A program may use at most 192 MiB of HBM per device.

v0:
```python
import jax
import jax.numpy as jnp
from jax import lax
from jax.sharding import PartitionSpec as P

H = 12
HEAD = 64
REACH = 2
WIN = 2560
eps_norm = 1e-06
masked_score = -1e30


def from_behind(value, axis, by):
    peers = lax.axis_size(axis)
    pairs = [(i, i + by) for i in range(peers) if 0 <= i + by < peers]
    return lax.ppermute(value, axis, pairs)


def dot_plain(matrix, factor):
    return jnp.dot(matrix, factor, preferred_element_type=jnp.float32)


def dot_rows(matrix, factor):
    return lax.dot_general(
        matrix, factor, (((0,), (0,)), ((), ())), preferred_element_type=jnp.float32
    )


def dot_cols(matrix, factor):
    return lax.dot_general(
        matrix, factor, (((1,), (1,)), ((), ())), preferred_element_type=jnp.float32
    )


def layer_norm(hidden, norm_gain, norm_shift):
    row_mean = jnp.mean(hidden, axis=1, keepdims=True)
    centred = hidden - row_mean
    row_var = jnp.mean(centred * centred, axis=1, keepdims=True)
    return centred * lax.rsqrt(row_var + eps_norm) * norm_gain + norm_shift


def gelu_exact(values):
    return jax.nn.gelu(values, approximate=False)


def segment_ids(row_lengths, first_row, num_rows):
    item_ends = jnp.cumsum(row_lengths, dtype=jnp.int32)
    places = first_row + jnp.arange(num_rows, dtype=jnp.int32)
    return jnp.sum(
        (places[:, None] >= item_ends[None, :]).astype(jnp.int32), axis=1, dtype=jnp.int32
    )


def split_heads(values):
    return values.reshape(values.shape[0], H, HEAD).transpose(1, 0, 2)


def join_heads(values):
    return values.transpose(1, 0, 2).reshape(values.shape[1], H * HEAD)


def widen_first(kv_pair):
    pieces = []
    for offset in range(-REACH, REACH + 1):
        if offset == 0:
            pieces.append(kv_pair)
        else:
            pieces.append(from_behind(kv_pair, "rows", -offset))
    return jnp.concatenate(pieces, axis=1)


def widen_again(kv_pair):
    pieces = []
    for offset in range(-REACH, REACH + 1):
        if offset == 0:
            pieces.append(kv_pair)
        else:
            pieces.append(from_behind(kv_pair, "rows", -offset))
    return jnp.concatenate(pieces, axis=1)


def collect(wide_grads):
    rows_dev = wide_grads.shape[1] // (2 * REACH + 1)
    summed = wide_grads[:, REACH * rows_dev : (REACH + 1) * rows_dev]
    for offset in range(-REACH, REACH + 1):
        if offset != 0:
            block_grads = wide_grads[
                :, (offset + REACH) * rows_dev : (offset + REACH + 1) * rows_dev
            ]
            summed = summed + from_behind(block_grads.astype(jnp.bfloat16), "rows", offset).astype(
                block_grads.dtype
            )
    return summed


def attend(query_rows, window, keep_mask):
    score_scale = HEAD ** (-0.5)

    def one_head(head_parts):
        head_query, head_keys, head_values = head_parts
        scores = jnp.where(keep_mask, dot_cols(head_query, head_keys) * score_scale, masked_score)
        row_max = jnp.max(scores, axis=1, keepdims=True)
        lifted = jnp.exp(scores - row_max)
        row_sum = jnp.sum(lifted, axis=1, keepdims=True)
        weights = (lifted / row_sum).astype(jnp.bfloat16)
        return (dot_plain(weights, head_values), (row_max + jnp.log(row_sum))[:, 0])

    outputs, logsum = lax.map(
        one_head, (split_heads(query_rows), split_heads(window[0]), split_heads(window[1]))
    )
    return (join_heads(outputs).astype(jnp.bfloat16), logsum)


def attend_back(query_rows, window, logsum, d_attended, keep_mask):
    score_scale = HEAD ** (-0.5)

    def one_head(head_parts):
        head_query, head_keys, head_values, head_logsum, head_grad = head_parts
        scores = jnp.where(keep_mask, dot_cols(head_query, head_keys) * score_scale, masked_score)
        weights = jnp.exp(scores - head_logsum[:, None])
        d_weights = dot_cols(head_grad, head_values)
        centre = jnp.sum(weights * d_weights, axis=1, keepdims=True)
        d_scores = (weights * (d_weights - centre)).astype(jnp.bfloat16)
        d_head_query = dot_plain(d_scores, head_keys) * score_scale
        d_head_keys = dot_rows(d_scores, head_query) * score_scale
        d_head_values = dot_rows(weights.astype(jnp.bfloat16), head_grad)
        return (d_head_query, d_head_keys, d_head_values)

    d_queries, d_keysets, d_valuesets = lax.map(
        one_head,
        (
            split_heads(query_rows),
            split_heads(window[0]),
            split_heads(window[1]),
            logsum,
            split_heads(d_attended),
        ),
    )
    return (
        join_heads(d_queries).astype(jnp.bfloat16),
        jnp.stack([join_heads(d_keysets), join_heads(d_valuesets)]),
    )


def forward(tokens, params, keep_mask, widen):
    (
        query_proj,
        key_proj,
        value_proj,
        query_bias,
        value_bias,
        output_proj,
        output_bias,
        attn_gain,
        attn_shift,
        hidden_proj,
        hidden_bias,
        return_proj,
        return_bias,
        final_gain,
        final_shift,
    ) = params
    query_rows = (dot_plain(tokens, query_proj) + query_bias.astype(jnp.float32)).astype(
        jnp.bfloat16
    )
    key_rows = dot_plain(tokens, key_proj).astype(jnp.bfloat16)
    value_rows = (dot_plain(tokens, value_proj) + value_bias.astype(jnp.float32)).astype(
        jnp.bfloat16
    )
    window = widen(jnp.stack([key_rows, value_rows]))
    attended, logsum = attend(query_rows, window, keep_mask)
    mixed = tokens.astype(jnp.float32) + (
        dot_plain(attended, output_proj) + output_bias.astype(jnp.float32)
    )
    normed = layer_norm(mixed, attn_gain.astype(jnp.float32), attn_shift.astype(jnp.float32))
    normed_low = normed.astype(jnp.bfloat16)
    hidden_pre = dot_plain(normed_low, hidden_proj) + hidden_bias.astype(jnp.float32)
    active = gelu_exact(hidden_pre).astype(jnp.bfloat16)
    second = normed + (dot_plain(active, return_proj) + return_bias.astype(jnp.float32))
    result = layer_norm(second, final_gain.astype(jnp.float32), final_shift.astype(jnp.float32))
    return (
        result,
        (
            query_rows,
            window,
            logsum,
            attended,
            mixed,
            normed,
            normed_low,
            hidden_pre,
            active,
            second,
        ),
    )


def backward(tokens, params, stored, out_grad, keep_mask):
    (
        query_proj,
        key_proj,
        value_proj,
        query_bias,
        value_bias,
        output_proj,
        output_bias,
        attn_gain,
        attn_shift,
        hidden_proj,
        hidden_bias,
        return_proj,
        return_bias,
        final_gain,
        final_shift,
    ) = params
    query_rows, window, logsum, attended, mixed, normed, normed_low, hidden_pre, active, second = (
        stored
    )
    ignored, final_back = jax.vjp(
        layer_norm, second, final_gain.astype(jnp.float32), final_shift.astype(jnp.float32)
    )
    d_second, grad_final_gain, grad_final_shift = final_back(out_grad.astype(jnp.float32))
    d_ffn = d_second.astype(jnp.bfloat16)
    grad_return_bias = jnp.sum(d_ffn.astype(jnp.float32), axis=0)
    grad_return_proj = dot_rows(active, d_ffn)
    ignored, gelu_back = jax.vjp(gelu_exact, hidden_pre)
    d_hidden = gelu_back(dot_cols(d_ffn, return_proj))[0].astype(jnp.bfloat16)
    grad_hidden_bias = jnp.sum(d_hidden.astype(jnp.float32), axis=0)
    grad_hidden_proj = dot_rows(normed_low, d_hidden)
    d_normed = dot_cols(d_hidden, hidden_proj) + d_second
    ignored, attn_back = jax.vjp(
        layer_norm, mixed, attn_gain.astype(jnp.float32), attn_shift.astype(jnp.float32)
    )
    d_mixed, grad_attn_gain, grad_attn_shift = attn_back(d_normed)
    d_branch = d_mixed.astype(jnp.bfloat16)
    grad_output_bias = jnp.sum(d_branch.astype(jnp.float32), axis=0)
    grad_output_proj = dot_rows(attended, d_branch)
    d_attended = dot_cols(d_branch, output_proj).astype(jnp.bfloat16)
    d_query, wide_grads = attend_back(query_rows, window, logsum, d_attended, keep_mask)
    key_value = collect(wide_grads)
    d_keys = key_value[0].astype(jnp.bfloat16)
    d_values = key_value[1].astype(jnp.bfloat16)
    grad_query_proj = dot_rows(tokens, d_query)
    grad_key_proj = dot_rows(tokens, d_keys)
    grad_value_proj = dot_rows(tokens, d_values)
    grad_query_bias = jnp.sum(d_query.astype(jnp.float32), axis=0)
    grad_value_bias = jnp.sum(d_values.astype(jnp.float32), axis=0)
    tokens_grad = (
        d_mixed
        + dot_cols(d_query, query_proj)
        + dot_cols(d_keys, key_proj)
        + dot_cols(d_values, value_proj)
    )
    return (
        tokens_grad,
        (
            grad_query_proj,
            grad_key_proj,
            grad_value_proj,
            grad_query_bias,
            grad_value_bias,
            grad_output_proj,
            grad_output_bias,
            grad_attn_gain,
            grad_attn_shift,
            grad_hidden_proj,
            grad_hidden_bias,
            grad_return_proj,
            grad_return_bias,
            grad_final_gain,
            grad_final_shift,
        ),
    )


def per_device(
    tokens,
    query_proj,
    key_proj,
    value_proj,
    query_bias,
    value_bias,
    output_proj,
    output_bias,
    attn_gain,
    attn_shift,
    hidden_proj,
    hidden_bias,
    return_proj,
    return_bias,
    final_gain,
    final_shift,
    item_lengths,
    out_grad,
):
    params = (
        lax.all_gather(query_proj, ("items", "rows"), axis=0, tiled=True),
        lax.all_gather(key_proj, ("items", "rows"), axis=0, tiled=True),
        lax.all_gather(value_proj, ("items", "rows"), axis=0, tiled=True),
        lax.all_gather(query_bias, ("items", "rows"), axis=0, tiled=True),
        lax.all_gather(value_bias, ("items", "rows"), axis=0, tiled=True),
        lax.all_gather(output_proj, ("items", "rows"), axis=0, tiled=True),
        lax.all_gather(output_bias, ("items", "rows"), axis=0, tiled=True),
        lax.all_gather(attn_gain, ("items", "rows"), axis=0, tiled=True),
        lax.all_gather(attn_shift, ("items", "rows"), axis=0, tiled=True),
        lax.all_gather(hidden_proj, ("items", "rows"), axis=0, tiled=True),
        lax.all_gather(hidden_bias, ("items", "rows"), axis=0, tiled=True),
        lax.all_gather(return_proj, ("items", "rows"), axis=0, tiled=True),
        lax.all_gather(return_bias, ("items", "rows"), axis=0, tiled=True),
        lax.all_gather(final_gain, ("items", "rows"), axis=0, tiled=True),
        lax.all_gather(final_shift, ("items", "rows"), axis=0, tiled=True),
    )
    rows_dev = tokens.shape[0]
    row_count = lax.axis_size("rows")
    position = lax.axis_index("rows") * rows_dev
    lengths_row = item_lengths[0]
    query_labels = segment_ids(lengths_row, position, rows_dev)
    window_first = position - REACH * rows_dev
    key_labels = segment_ids(lengths_row, window_first, WIN)
    key_places = window_first + jnp.arange(WIN, dtype=jnp.int32)
    inside = (key_places >= 0) & (key_places < row_count * rows_dev)
    keep_mask = (query_labels[:, None] == key_labels[None, :]) & inside[None, :]
    result, stored = forward(tokens, params, keep_mask, widen_first)
    fresh = lax.optimization_barrier((tokens, params, result))
    ignored, stored = forward(fresh[0], fresh[1], keep_mask, widen_again)
    tokens_grad, local_grads = backward(tokens, params, stored, out_grad, keep_mask)
    (
        grad_query_proj,
        grad_key_proj,
        grad_value_proj,
        grad_query_bias,
        grad_value_bias,
        grad_output_proj,
        grad_output_bias,
        grad_attn_gain,
        grad_attn_shift,
        grad_hidden_proj,
        grad_hidden_bias,
        grad_return_proj,
        grad_return_bias,
        grad_final_gain,
        grad_final_shift,
    ) = local_grads
    summed_grads = (
        lax.psum_scatter(grad_query_proj, ("items", "rows"), scatter_dimension=0, tiled=True),
        lax.psum_scatter(grad_key_proj, ("items", "rows"), scatter_dimension=0, tiled=True),
        lax.psum_scatter(grad_value_proj, ("items", "rows"), scatter_dimension=0, tiled=True),
        lax.psum_scatter(grad_query_bias, ("items", "rows"), scatter_dimension=0, tiled=True),
        lax.psum_scatter(grad_value_bias, ("items", "rows"), scatter_dimension=0, tiled=True),
        lax.psum_scatter(grad_output_proj, ("items", "rows"), scatter_dimension=0, tiled=True),
        lax.psum_scatter(grad_output_bias, ("items", "rows"), scatter_dimension=0, tiled=True),
        lax.psum_scatter(grad_attn_gain, ("items", "rows"), scatter_dimension=0, tiled=True),
        lax.psum_scatter(grad_attn_shift, ("items", "rows"), scatter_dimension=0, tiled=True),
        lax.psum_scatter(grad_hidden_proj, ("items", "rows"), scatter_dimension=0, tiled=True),
        lax.psum_scatter(grad_hidden_bias, ("items", "rows"), scatter_dimension=0, tiled=True),
        lax.psum_scatter(grad_return_proj, ("items", "rows"), scatter_dimension=0, tiled=True),
        lax.psum_scatter(grad_return_bias, ("items", "rows"), scatter_dimension=0, tiled=True),
        lax.psum_scatter(grad_final_gain, ("items", "rows"), scatter_dimension=0, tiled=True),
        lax.psum_scatter(grad_final_shift, ("items", "rows"), scatter_dimension=0, tiled=True),
    )
    return (
        result.astype(jnp.bfloat16),
        tokens_grad,
        summed_grads[0],
        summed_grads[1],
        summed_grads[2],
        summed_grads[3],
        summed_grads[4],
        summed_grads[5],
        summed_grads[6],
        summed_grads[7],
        summed_grads[8],
        summed_grads[9],
        summed_grads[10],
        summed_grads[11],
        summed_grads[12],
        summed_grads[13],
        summed_grads[14],
    )


def solution(mesh):
    return jax.shard_map(
        per_device,
        mesh=mesh,
        in_specs=(
            P(("items", "rows"), None),
            P(("items", "rows"), None),
            P(("items", "rows"), None),
            P(("items", "rows"), None),
            P(("items", "rows")),
            P(("items", "rows")),
            P(("items", "rows"), None),
            P(("items", "rows")),
            P(("items", "rows")),
            P(("items", "rows")),
            P(("items", "rows"), None),
            P(("items", "rows")),
            P(("items", "rows"), None),
            P(("items", "rows")),
            P(("items", "rows")),
            P(("items", "rows")),
            P("items", None),
            P(("items", "rows"), None),
        ),
        out_specs=(
            P(("items", "rows"), None),
            P(("items", "rows"), None),
            P(("items", "rows"), None),
            P(("items", "rows"), None),
            P(("items", "rows"), None),
            P(("items", "rows")),
            P(("items", "rows")),
            P(("items", "rows"), None),
            P(("items", "rows")),
            P(("items", "rows")),
            P(("items", "rows")),
            P(("items", "rows"), None),
            P(("items", "rows")),
            P(("items", "rows"), None),
            P(("items", "rows")),
            P(("items", "rows")),
            P(("items", "rows")),
        ),
        check_vma=False,
    )
```

profile of v0, /device:TPU:0, one launch (start us, length us, event | category | flops | bytes accessed | tf_op | source)
XLA Modules:
  0.0 1466.5 jit_solution(15196208716803237145)
XLA Ops:
  18.2 42.3 %all-reduce.19 = (bf16[3072]{0:T(1024)(128)(2,1)S(1)}, bf16[768]{0:T(1024)(128)(2,1)S(1)}, bf16[768]{0:T(1024)(128)(2,1)S(1)}, bf16[768]{0:T(1024)(128)(2,1)S(1)...) all-reduce(bf16[3072]{0:T(1024)(128)(2,1)S(1)} %dynamic-update-slic, ...), channel_id=1, replica_groups=mesh['items'=4,'rows'=8] {'items','rows'}, use_global_device_ids=true, to_apply=%add.5 | all-reduce | flops 9216 | bytes 36864
  70.2 53.8 %all-gather.11.cloned.1.call-done = bf16[768,768]{1,0:T(8,128)(2,1)} async-done(((bf16[24,768]{1,0:T(8,128)(2,1)}), bf16[768,768]{1,0:T(8,128)(2,1)}) %all-gather.11.cloned.1.call-update) | async-done | bytes 1179664 | tf_op jit(solution)/shard_map/all_gather | solution.py:300
  138.7 74.1 %all-gather.7.cloned.1.call-done = bf16[768,768]{1,0:T(8,128)(2,1)} async-done(((bf16[24,768]{1,0:T(8,128)(2,1)}), bf16[768,768]{1,0:T(8,128)(2,1)}) %all-gather.7.cloned.1.call-update) | async-done | bytes 1179664 | tf_op jit(solution)/shard_map/all_gather | solution.py:298
  239.3 66.2 %while.39 = (s32[]{:T(128)}, bf16[12,512,64]{1,2,0:T(8,128)(2,1)S(1)}, bf16[12,512,64]{1,2,0:T(8,128)(2,1)S(1)}, bf16[12,2560,64]{1,2,0:T(8,128)(2,1)}, bf16[12,...) while((s32[]{:T(128)}, ...), condition=%wide.region_6.7_spmd.clone, body=%wide.region_3.6_spmd.clone.sunk | while | flops 348650496 | bytes 16610397 | solution.py:109
  309.3 25.0 %all-gather.15.cloned.1.call-done = bf16[768,3072]{1,0:T(8,128)(2,1)} async-done(((bf16[24,3072]{1,0:T(8,128)(2,1)}), bf16[768,3072]{1,0:T(8,128)(2,1)}) %all-gather.15.cloned.1.call-update) | async-done | bytes 4718608 | tf_op jit(solution)/shard_map/all_gather | solution.py:307
  334.3 64.6 %all-gather.17.cloned.1.call-done = bf16[3072,768]{1,0:T(8,128)(2,1)} async-done(((bf16[96,768]{1,0:T(8,128)(2,1)}), bf16[3072,768]{1,0:T(8,128)(2,1)}) %all-gather.17.cloned.1.call-update) | async-done | bytes 4718608 | tf_op jit(solution)/shard_map/all_gather | solution.py:309
  398.9 22.1 %fusion.146 = (f32[512]{0:T(512)S(1)}, f32[512,768]{1,0:T(8,128)S(1)}) fusion(f32[768]{0:T(1024)S(1)} %convert_element_type.209, bf16[3072,768]{1,0:T(8,128)(2,1)} %all-gather.17.cloned.1.call-done, bf16[768,3072]{1,0:T(8,128)(2,1)} %all-gather.15.cloned.1.call-done, f32[3072]{0:T(1024)S(1)} %convert_element_type.207, f32[512,768]{1,0:T(8,128)} %copy-done.14, ...), kind=kOutput, calls=%fused_computation.239 | convolution fusion | flops 4940365312 | bytes 12610560 | tf_op jit(solution)/shard_map/dot_general | solution.py:21
  439.6 23.8 %collective-permute-done.4 = bf16[2,512,768]{2,1,0:T(8,128)(2,1)} collective-permute-done((bf16[2,512,768]{2,1,0:T(8,128)(2,1)}, bf16[2,512,768]{2,1,0:T(8,128)(2,1)}, u32[]{:S(2)}, u32[]{:S(2)}) %collective-permute-start.4) | collective-permute-done | bytes 1572896 | tf_op jit(solution)/shard_map/ppermute | solution.py:17
  464.9 36.5 %collective-permute-done.5 = bf16[2,512,768]{2,1,0:T(8,128)(2,1)} collective-permute-done((bf16[2,512,768]{2,1,0:T(8,128)(2,1)}, bf16[2,512,768]{2,1,0:T(8,128)(2,1)}, u32[]{:S(2)}, u32[]{:S(2)}) %collective-permute-start.5) | collective-permute-done | bytes 1572896 | tf_op jit(solution)/shard_map/ppermute | solution.py:17
  516.2 8.2 copy.95
  530.7 8.3 copy.96
  539.0 115.3 %while.40 = (s32[]{:T(128)}, bf16[12,512,64]{1,2,0:T(8,128)(2,1)S(1)}, f32[12,512]{1,0:T(8,128)S(1)}, bf16[12,512,64]{2,1,0:T(8,128)(2,1)S(1)}, bf16[12,2560,64]...) while((s32[]{:T(128)}, ...), condition=%wide.region_14.15_spmd.clone, body=%wide.region_11.14_spmd.clone.sunk | while | flops 348651008 | bytes 38313100 | solution.py:109
  657.8 20.1 %multiply_convert_fusion.1 = (bf16[512,3072]{1,0:T(8,128)(2,1)S(1)}, f32[512,3072]{1,0:T(8,128)}, f32[512,3072]{1,0:T(8,128)}) fusion(f32[3072]{0:T(1024)S(1)} %convert_element_type.226, bf16[768,3072]{1,0:T(8,128)(2,1)} %all-gather.15.cloned.1.call-done, f32[512,768]{1,0:T(8,128)S(1)} %get-tuple-element.516, f32[768]{0:T(1024)S(1)} %convert_element_type.224, ...), kind=kOutput, calls=%fused_computation.79 | convolution fusion | flops 2521694208 | bytes 22042624 | tf_op jit(solution)/shard_map/dot_general | solution.py:21
  682.8 8.3 convert_reduce_fusion
  703.1 151.0 %while.41 = (s32[]{:T(128)}, bf16[12,512,64]{1,2,0:T(8,128)(2,1)S(1)}, f32[12,2560,64]{1,2,0:T(8,128)}, f32[12,2560,64]{1,2,0:T(8,128)}, bf16[12,512,64]{2,1,0:T...) while((s32[]{:T(128)}, ...), condition=%wide.region_25.26_spmd.clone, body=%wide.region_23.25_spmd.clone.sunk | while | flops 853474816 | bytes 43153024 | solution.py:130
  859.5 9.8 fusion.56
  880.8 32.7 %collective-permute-done.10 = bf16[2,512,768]{1,2,0:T(8,128)(2,1)S(1)} collective-permute-done((bf16[2,512,768]{1,2,0:T(8,128)(2,1)S(1)}, bf16[2,512,768]{1,2,0:T(8,128)(2,1)S(1)}, u32[]{:S(2)}, u32[]{:S(2)}) %collective-permute-start.10) | collective-permute-done | bytes 1572896 | tf_op jit(solution)/shard_map/ppermute | solution.py:17
  936.2 8.4 fusion.153
  944.6 8.9 fusion.133
  958.6 76.0 %all-reduce.18 = (f32[768]{0:T(1024)S(1)}, f32[768]{0:T(1024)S(1)}, f32[768]{0:T(1024)S(1)}, f32[768]{0:T(1024)S(1)}, f32[768]{0:T(1024)S(1)}, /*index=5*/f32[30...) all-reduce(f32[768]{0:T(1024)S(1)} %reduce_sum.291, ...), channel_id=5, replica_groups=mesh['items'=4,'rows'=8] {'items','rows'}, use_global_device_ids=true, to_apply=%region_30.31.clone | all-reduce | flops 9216 | bytes 73728
  1044.3 27.5 %reduce-scatter.21.cloned.1.call-done = f32[24,768]{1,0:T(8,128)} async-done(((f32[768,768]{1,0:T(8,128)}), f32[24,768]{1,0:T(8,128)}) %reduce-scatter.21.cloned.1.call-update) | async-done | bytes 73744
  1071.8 104.4 %reduce-scatter.23.cloned.1.call-done = f32[24,768]{1,0:T(8,128)} async-done(((f32[768,768]{1,0:T(8,128)}), f32[24,768]{1,0:T(8,128)}) %reduce-scatter.23.cloned.1.call-update) | async-done | bytes 73744
  1176.1 141.8 %reduce-scatter.17.cloned.1.call-done = f32[96,768]{1,0:T(8,128)} async-done(((f32[3072,768]{1,0:T(8,128)}), f32[96,768]{1,0:T(8,128)}) %reduce-scatter.17.cloned.1.call-update) | async-done | bytes 294928 | tf_op jit(solution)/shard_map/reduce_scatter | solution.py:357
  1317.9 141.5 %reduce-scatter.15.cloned.1.call-done = f32[24,3072]{1,0:T(8,128)} async-done(((f32[768,3072]{1,0:T(8,128)}), f32[24,3072]{1,0:T(8,128)}) %reduce-scatter.15.cloned.1.call-update) | async-done | bytes 294928 | tf_op jit(solution)/shard_map/reduce_scatter | solution.py:355
  (432 shorter events, 511.3 us)
Async XLA Ops:
  7.2 60.7 %all-gather.9.cloned.1.call-start = ((), (), s32[]{:S(2)}) async-start(), calls=%async_computation.7 | async-start | bytes 1216512 | tf_op jit(solution)/shard_map/all_gather | solution.py:299
  7.9 116.1 %all-gather.11.cloned.1.call-start = ((), (), s32[]{:S(2)}) async-start(), calls=%async_computation.8 | async-start | bytes 1216512 | tf_op jit(solution)/shard_map/all_gather | solution.py:300
  8.7 204.1 %all-gather.7.cloned.1.call-start = ((), (), s32[]{:S(2)}) async-start(), calls=%async_computation.6 | async-start | bytes 1216512 | tf_op jit(solution)/shard_map/all_gather | solution.py:298
  9.4 296.2 %all-gather.13.cloned.1.call-start = ((), (), s32[]{:S(2)}) async-start(), calls=%async_computation.9 | async-start | bytes 1216512 | tf_op jit(solution)/shard_map/all_gather | solution.py:303
  10.0 324.3 %all-gather.15.cloned.1.call-start = ((), (), s32[]{:S(2)}) async-start(), calls=%async_computation.10 | async-start | bytes 4866048 | tf_op jit(solution)/shard_map/all_gather | solution.py:307
  10.6 388.3 %all-gather.17.cloned.1.call-start = ((), (), s32[]{:S(2)}) async-start(), calls=%async_computation.11 | async-start | bytes 4866048 | tf_op jit(solution)/shard_map/all_gather | solution.py:309
  127.4 89.8 %collective-permute-start = (bf16[2,512,768]{2,1,0:T(8,128)(2,1)}, bf16[2,512,768]{2,1,0:T(8,128)(2,1)}, u32[]{:S(2)}, u32[]{:S(2)}) collective-permute-start(bf16[2,512,768]{2,1,0:T(8,128)(2,1)} %pad_maximum_fusion.1), channel_id=1, source_target_pairs={{0,2},{1,3},{2,4},{3,5},{4,6},{5,7},{8,10},{9,11},{10,12},{11,13},... | collective-permute-start | bytes 4718600 | tf_op jit(solution)/shard_map/ppermute | solution.py:17
  131.0 87.7 %collective-permute-start.1 = (bf16[2,512,768]{2,1,0:T(8,128)(2,1)}, bf16[2,512,768]{2,1,0:T(8,128)(2,1)}, u32[]{:S(2)}, u32[]{:S(2)}) collective-permute-start(bf16[2,512,768]{2,1,0:T(8,128)(2,1)} %pad_maximum_fusion.1), channel_id=1, source_target_pairs={{0,1},{1,2},{2,3},{3,4},{4,5},{5,6},{6,7},{8,9},{9,10},{10,11},{11... | collective-permute-start | bytes 4718600 | tf_op jit(solution)/shard_map/ppermute | solution.py:17
  135.5 84.8 %collective-permute-start.2 = (bf16[2,512,768]{2,1,0:T(8,128)(2,1)}, bf16[2,512,768]{2,1,0:T(8,128)(2,1)}, u32[]{:S(2)}, u32[]{:S(2)}) collective-permute-start(bf16[2,512,768]{2,1,0:T(8,128)(2,1)} %pad_maximum_fusion.1), channel_id=1, source_target_pairs={{1,0},{2,1},{3,2},{4,3},{5,4},{6,5},{7,6},{9,8},{10,9},{11,10},{12... | collective-permute-start | bytes 4718600 | tf_op jit(solution)/shard_map/ppermute | solution.py:17
  136.8 85.0 %collective-permute-start.3 = (bf16[2,512,768]{2,1,0:T(8,128)(2,1)}, bf16[2,512,768]{2,1,0:T(8,128)(2,1)}, u32[]{:S(2)}, u32[]{:S(2)}) collective-permute-start(bf16[2,512,768]{2,1,0:T(8,128)(2,1)} %pad_maximum_fusion.1), channel_id=1, source_target_pairs={{2,0},{3,1},{4,2},{5,3},{6,4},{7,5},{10,8},{11,9},{12,10},{13,11},... | collective-permute-start | bytes 4718600 | tf_op jit(solution)/shard_map/ppermute | solution.py:17
  138.1 906.2 %reduce-scatter.13.cloned.1.call-start = ((), (), s32[]{:S(2)}) async-start(), calls=%async_computation.12 | async-start | bytes 2433024 | tf_op jit(solution)/shard_map/reduce_scatter | solution.py:351
  425.7 37.7 %collective-permute-start.4 = (bf16[2,512,768]{2,1,0:T(8,128)(2,1)}, bf16[2,512,768]{2,1,0:T(8,128)(2,1)}, u32[]{:S(2)}, u32[]{:S(2)}) collective-permute-start(bf16[2,512,768]{2,1,0:T(8,128)(2,1)} %pad_maximum_fusion.2), channel_id=1, source_target_pairs={{0,2},{1,3},{2,4},{3,5},{4,6},{5,7},{8,10},{9,11},{10,12},{11,13},... | collective-permute-start | bytes 4718600 | tf_op jit(solution)/shard_map/ppermute | solution.py:17
  430.1 71.2 %collective-permute-start.5 = (bf16[2,512,768]{2,1,0:T(8,128)(2,1)}, bf16[2,512,768]{2,1,0:T(8,128)(2,1)}, u32[]{:S(2)}, u32[]{:S(2)}) collective-permute-start(bf16[2,512,768]{2,1,0:T(8,128)(2,1)} %pad_maximum_fusion.2), channel_id=1, source_target_pairs={{0,1},{1,2},{2,3},{3,4},{4,5},{5,6},{6,7},{8,9},{9,10},{10,11},{11... | collective-permute-start | bytes 4718600 | tf_op jit(solution)/shard_map/ppermute | solution.py:17
  434.7 68.4 %collective-permute-start.6 = (bf16[2,512,768]{2,1,0:T(8,128)(2,1)}, bf16[2,512,768]{2,1,0:T(8,128)(2,1)}, u32[]{:S(2)}, u32[]{:S(2)}) collective-permute-start(bf16[2,512,768]{2,1,0:T(8,128)(2,1)} %pad_maximum_fusion.2), channel_id=1, source_target_pairs={{1,0},{2,1},{3,2},{4,3},{5,4},{6,5},{7,6},{9,8},{10,9},{11,10},{12... | collective-permute-start | bytes 4718600 | tf_op jit(solution)/shard_map/ppermute | solution.py:17
  436.0 69.2 %collective-permute-start.7 = (bf16[2,512,768]{2,1,0:T(8,128)(2,1)}, bf16[2,512,768]{2,1,0:T(8,128)(2,1)}, u32[]{:S(2)}, u32[]{:S(2)}) collective-permute-start(bf16[2,512,768]{2,1,0:T(8,128)(2,1)} %pad_maximum_fusion.2), channel_id=1, source_target_pairs={{2,0},{3,1},{4,2},{5,3},{6,4},{7,5},{10,8},{11,9},{12,10},{13,11},... | collective-permute-start | bytes 4718600 | tf_op jit(solution)/shard_map/ppermute | solution.py:17
  697.7 346.7 %reduce-scatter.19.cloned.1.call-start = ((), (), s32[]{:S(2)}) async-start(), calls=%async_computation.15 | async-start | bytes 2433024
  859.5 212.3 %reduce-scatter.21.cloned.1.call-start = ((), (), s32[]{:S(2)}) async-start(), calls=%async_computation.16 | async-start | bytes 2433024
  872.7 40.8 %collective-permute-start.10 = (bf16[2,512,768]{1,2,0:T(8,128)(2,1)S(1)}, bf16[2,512,768]{1,2,0:T(8,128)(2,1)S(1)}, u32[]{:S(2)}, u32[]{:S(2)}) collective-permute-start(bf16[2,512,768]{1,2,0:T(8,128)(2,1)S(1)} %get-tuple-element.505), channel_id=1, source_target_pairs={{0,1},{1,2},{2,3},{3,4},{4,5},{5,6},{6,7},{8,9},{9,10},{10,11},{11... | collective-permute-start | bytes 4718600 | tf_op jit(solution)/shard_map/ppermute | solution.py:17
  876.6 37.2 %collective-permute-start.11 = (bf16[2,512,768]{1,2,0:T(8,128)(2,1)S(1)}, bf16[2,512,768]{1,2,0:T(8,128)(2,1)S(1)}, u32[]{:S(2)}, u32[]{:S(2)}) collective-permute-start(bf16[2,512,768]{1,2,0:T(8,128)(2,1)S(1)} %get-tuple-element.504), channel_id=1, source_target_pairs={{0,2},{1,3},{2,4},{3,5},{4,6},{5,7},{8,10},{9,11},{10,12},{11,13},... | collective-permute-start | bytes 4718600 | tf_op jit(solution)/shard_map/ppermute | solution.py:17
  878.1 42.8 %collective-permute-start.8 = (bf16[2,512,768]{1,2,0:T(8,128)(2,1)S(1)}, bf16[2,512,768]{1,2,0:T(8,128)(2,1)S(1)}, u32[]{:S(2)}, u32[]{:S(2)}) collective-permute-start(bf16[2,512,768]{1,2,0:T(8,128)(2,1)S(1)} %get-tuple-element.503), channel_id=1, source_target_pairs={{2,0},{3,1},{4,2},{5,3},{6,4},{7,5},{10,8},{11,9},{12,10},{13,11},... | collective-permute-start | bytes 4718600 | tf_op jit(solution)/shard_map/ppermute | solution.py:17
  879.4 41.5 %collective-permute-start.9 = (bf16[2,512,768]{1,2,0:T(8,128)(2,1)S(1)}, bf16[2,512,768]{1,2,0:T(8,128)(2,1)S(1)}, u32[]{:S(2)}, u32[]{:S(2)}) collective-permute-start(bf16[2,512,768]{1,2,0:T(8,128)(2,1)S(1)} %get-tuple-element.506), channel_id=1, source_target_pairs={{1,0},{2,1},{3,2},{4,3},{5,4},{6,5},{7,6},{9,8},{10,9},{11,10},{12... | collective-permute-start | bytes 4718600 | tf_op jit(solution)/shard_map/ppermute | solution.py:17
  929.4 246.7 %reduce-scatter.23.cloned.1.call-start = ((), (), s32[]{:S(2)}) async-start(), calls=%async_computation.17 | async-start | bytes 2433024
  935.9 382.0 %reduce-scatter.17.cloned.1.call-start = ((), (), s32[]{:S(2)}) async-start(), calls=%async_computation.14 | async-start | bytes 9732096 | tf_op jit(solution)/shard_map/reduce_scatter | solution.py:357
  944.6 514.8 %reduce-scatter.15.cloned.1.call-start = ((), (), s32[]{:S(2)}) async-start(), calls=%async_computation.13 | async-start | bytes 9732096 | tf_op jit(solution)/shard_map/reduce_scatter | solution.py:355
  (38 other events, 589.4 us)
Sparse Core Ops, SparseCore 0:
  10.9 56.9 all-gather.8
  70.8 53.1 all-gather.10
  127.0 85.7 all-gather.6
  215.6 53.3 all-gather.12
  271.7 62.5 all-gather.14
  337.0 61.8 all-gather.16
  697.8 97.2 reduce-scatter.12
  859.6 107.6 reduce-scatter.18
  973.2 98.5 reduce-scatter.20
  1077.5 98.6 reduce-scatter.22
  1182.6 135.2 reduce-scatter.16
  1324.2 135.1 reduce-scatter.14
where the time goes:
time: 1480 us; the launch traced here: 1470 us
  waiting for transfers between devices  744 us (50%)
  matrix products  386 us (26%)
  local copies, waits for them, and re-layouts  121 us (8%)
  blocking collectives  118 us (8%)
  other arithmetic  49.4 us (3%)
  starting transfers between devices  31.1 us (2%)
  between operations  15.4 us (1%)
    dot_general x47, matrix products, dot_plain(): return jnp.dot(matrix, factor, preferred_element_type=jnp.float32)  155 us
    dot_general x54, matrix products, dot_cols(): lax.dot_general(matrix, factor, (((1,), (1,)), ((), ())), preferred_eleme...  148 us
    reduce_scatter x1, waiting for transfers between devices, per_device(): lax.psum_scatter(grad_return_proj, ('items', 'rows'), scatter_dimension=0...  142 us
    reduce_scatter x1, waiting for transfers between devices, per_device(): lax.psum_scatter(grad_hidden_proj, ('items', 'rows'), scatter_dimension=0...  142 us
    unnamed x15, waiting for transfers between devices  135 us
    unnamed x2, blocking collectives  118 us
    ppermute x12, waiting for transfers between devices, from_behind(): return lax.ppermute(value, axis, pairs)  101 us
    dot_general x30, matrix products, dot_rows(): lax.dot_general(matrix, factor, (((0,), (0,)), ((), ())), preferred_eleme...  82.9 us
  transfers between devices with their start and end apart: 24, of which 15 were waited for; matrix products, arithmetic and copies ran while one was open for 23% of the time, Pallas kernels for 0%

commit v1 on v0

--- a/solution.py
+++ b/solution.py
@@ -297,7 +297,12 @@
     params = (
         lax.all_gather(query_proj, ("items", "rows"), axis=0, tiled=True),
         lax.all_gather(key_proj, ("items", "rows"), axis=0, tiled=True),
-        lax.all_gather(value_proj, ("items", "rows"), axis=0, tiled=True),
+        jnp.concatenate(
+            lax.all_to_all(
+                jnp.stack([value_proj] * lax.axis_size(("items", "rows"))), ("items", "rows"), 0, 0
+            ),
+            axis=0,
+        ),
         lax.all_gather(query_bias, ("items", "rows"), axis=0, tiled=True),
         lax.all_gather(value_bias, ("items", "rows"), axis=0, tiled=True),
         lax.all_gather(output_proj, ("items", "rows"), axis=0, tiled=True),

time: 1480 us -> 1430 us (0.966)
  waiting for transfers between devices: 744 us -> 681 us
    all_gather x1 -> x0, waiting for transfers between devices: 53.8 us -> none  [per_device(): lax.all_gather(value_proj, ('items', 'rows'), axis=0, tiled=True)]
    unnamed x91 -> x97, local copies, waits for them, and re-layouts: 50.3 us -> 51.2 us
    unnamed x15 -> x14, waiting for transfers between devices: 135 us -> 135 us
  transfers between devices with their start and end apart: 24 -> 24, of which waited for: 15 -> 14; matrix products, arithmetic and copies ran while one was open for 23% -> 24% of each run, Pallas kernels for 0% -> 0%
where the time goes in v1:
time: 1430 us; the launch traced here: 1410 us
  waiting for transfers between devices  681 us (48%)
  matrix products  385 us (27%)
  local copies, waits for them, and re-layouts  125 us (9%)
  blocking collectives  120 us (8%)
  other arithmetic  49.3 us (3%)
  starting transfers between devices  38.4 us (3%)
  between operations  15.1 us (1%)
    dot_general x47, matrix products, dot_plain(): return jnp.dot(matrix, factor, preferred_element_type=jnp.float32)  154 us
    dot_general x54, matrix products, dot_cols(): lax.dot_general(matrix, factor, (((1,), (1,)), ((), ())), preferred_eleme...  148 us
    reduce_scatter x1, waiting for transfers between devices, per_device(): lax.psum_scatter(grad_hidden_proj, ('items', 'rows'), scatter_dimension=0...  142 us
    reduce_scatter x1, waiting for transfers between devices, per_device(): lax.psum_scatter(grad_return_proj, ('items', 'rows'), scatter_dimension=0...  142 us
    unnamed x14, waiting for transfers between devices  135 us
    unnamed x2, blocking collectives  120 us
    ppermute x12, waiting for transfers between devices, from_behind(): return lax.ppermute(value, axis, pairs)  101 us
    dot_general x30, matrix products, dot_rows(): lax.dot_general(matrix, factor, (((0,), (0,)), ((), ())), preferred_eleme...  82.9 us
  transfers between devices with their start and end apart: 24, of which 14 were waited for; matrix products, arithmetic and copies ran while one was open for 24% of the time, Pallas kernels for 0%

profile of v1, /device:TPU:0, one launch (start us, length us, event | category | flops | bytes accessed | tf_op | source)
XLA Modules:
  0.0 1414.5 jit_solution(9441752144360628107)
XLA Ops:
  11.8 7.3 all-to-all-start
  26.8 43.6 %all-reduce.19 = (bf16[3072]{0:T(1024)(128)(2,1)S(1)}, bf16[768]{0:T(1024)(128)(2,1)S(1)}, bf16[768]{0:T(1024)(128)(2,1)S(1)}, bf16[768]{0:T(1024)(128)(2,1)S(1)...) all-reduce(bf16[3072]{0:T(1024)(128)(2,1)S(1)} %dynamic-update-slic, ...), channel_id=1, replica_groups=mesh['items'=4,'rows'=8] {'items','rows'}, use_global_device_ids=true, to_apply=%add.5 | all-reduce | flops 9216 | bytes 36864
  87.4 73.8 %all-gather.6.cloned.1.call-done = bf16[768,768]{1,0:T(8,128)(2,1)} async-done(((bf16[24,768]{1,0:T(8,128)(2,1)}), bf16[768,768]{1,0:T(8,128)(2,1)}) %all-gather.6.cloned.1.call-update) | async-done | bytes 1179664 | tf_op jit(solution)/shard_map/all_gather | solution.py:298
  188.8 66.8 %while.39 = (s32[]{:T(128)}, bf16[12,512,64]{1,2,0:T(8,128)(2,1)S(1)}, bf16[12,512,64]{1,2,0:T(8,128)(2,1)}, bf16[12,2560,64]{1,2,0:T(8,128)(2,1)}, bf16[12,2560...) while((s32[]{:T(128)}, ...), condition=%wide.region_6.7_spmd.clone, body=%wide.region_3.6_spmd.clone.sunk | while | flops 348650496 | bytes 16607837 | solution.py:109
  259.2 23.1 %all-gather.12.cloned.1.call-done = bf16[768,3072]{1,0:T(8,128)(2,1)} async-done(((bf16[24,3072]{1,0:T(8,128)(2,1)}), bf16[768,3072]{1,0:T(8,128)(2,1)}) %all-gather.12.cloned.1.call-update) | async-done | bytes 4718608 | tf_op jit(solution)/shard_map/all_gather | solution.py:312
  282.3 64.6 %all-gather.14.cloned.1.call-done = bf16[3072,768]{1,0:T(8,128)(2,1)} async-done(((bf16[96,768]{1,0:T(8,128)(2,1)}), bf16[3072,768]{1,0:T(8,128)(2,1)}) %all-gather.14.cloned.1.call-update) | async-done | bytes 4718608 | tf_op jit(solution)/shard_map/all_gather | solution.py:314
  346.9 22.1 %fusion.151 = (f32[512]{0:T(512)S(1)}, f32[512,768]{1,0:T(8,128)S(1)}) fusion(f32[768]{0:T(1024)S(1)} %convert_element_type.212, bf16[3072,768]{1,0:T(8,128)(2,1)} %all-gather.14.cloned.1.call-done, bf16[768,3072]{1,0:T(8,128)(2,1)} %all-gather.12.cloned.1.call-done, f32[3072]{0:T(1024)S(1)} %convert_element_type.210, f32[512,768]{1,0:T(8,128)} %copy-done.19, ...), kind=kOutput, calls=%fused_computation.240 | convolution fusion | flops 4940365312 | bytes 12610560 | tf_op jit(solution)/shard_map/dot_general | solution.py:21
  387.6 23.8 %collective-permute-done.4 = bf16[2,512,768]{2,1,0:T(8,128)(2,1)} collective-permute-done((bf16[2,512,768]{2,1,0:T(8,128)(2,1)}, bf16[2,512,768]{2,1,0:T(8,128)(2,1)}, u32[]{:S(2)}, u32[]{:S(2)}) %collective-permute-start.4) | collective-permute-done | bytes 1572896 | tf_op jit(solution)/shard_map/ppermute | solution.py:17
  412.9 36.5 %collective-permute-done.5 = bf16[2,512,768]{2,1,0:T(8,128)(2,1)} collective-permute-done((bf16[2,512,768]{2,1,0:T(8,128)(2,1)}, bf16[2,512,768]{2,1,0:T(8,128)(2,1)}, u32[]{:S(2)}, u32[]{:S(2)}) %collective-permute-start.5) | collective-permute-done | bytes 1572896 | tf_op jit(solution)/shard_map/ppermute | solution.py:17
  464.2 8.2 copy.95
  478.7 8.3 copy.96
  487.0 115.3 %while.40 = (s32[]{:T(128)}, bf16[12,512,64]{1,2,0:T(8,128)(2,1)S(1)}, f32[12,512]{1,0:T(8,128)S(1)}, bf16[12,512,64]{2,1,0:T(8,128)(2,1)S(1)}, bf16[12,2560,64]...) while((s32[]{:T(128)}, ...), condition=%wide.region_14.15_spmd.clone, body=%wide.region_11.14_spmd.clone.sunk | while | flops 348651008 | bytes 38313100 | solution.py:109
  605.8 20.1 %multiply_convert_fusion.1 = (bf16[512,3072]{1,0:T(8,128)(2,1)S(1)}, f32[512,3072]{1,0:T(8,128)}, f32[512,3072]{1,0:T(8,128)}) fusion(f32[3072]{0:T(1024)S(1)} %convert_element_type.229, bf16[768,3072]{1,0:T(8,128)(2,1)} %all-gather.12.cloned.1.call-done, f32[512,768]{1,0:T(8,128)S(1)} %get-tuple-element.516, f32[768]{0:T(1024)S(1)} %convert_element_type.227, ...), kind=kOutput, calls=%fused_computation.79 | convolution fusion | flops 2521694208 | bytes 22042624 | tf_op jit(solution)/shard_map/dot_general | solution.py:21
  630.8 8.3 convert_reduce_fusion
  651.1 151.2 %while.41 = (s32[]{:T(128)}, bf16[12,512,64]{1,2,0:T(8,128)(2,1)S(1)}, f32[12,2560,64]{1,2,0:T(8,128)}, f32[12,2560,64]{1,2,0:T(8,128)}, bf16[12,512,64]{2,1,0:T...) while((s32[]{:T(128)}, ...), condition=%wide.region_25.26_spmd.clone, body=%wide.region_23.25_spmd.clone.sunk | while | flops 853474816 | bytes 43153024 | solution.py:130
  807.7 9.8 fusion.56
  829.1 32.6 %collective-permute-done.10 = bf16[2,512,768]{1,2,0:T(8,128)(2,1)S(1)} collective-permute-done((bf16[2,512,768]{1,2,0:T(8,128)(2,1)S(1)}, bf16[2,512,768]{1,2,0:T(8,128)(2,1)S(1)}, u32[]{:S(2)}, u32[]{:S(2)}) %collective-permute-start.10) | collective-permute-done | bytes 1572896 | tf_op jit(solution)/shard_map/ppermute | solution.py:17
  884.4 8.4 fusion.158
  892.9 8.9 fusion.138
  906.9 75.9 %all-reduce.18 = (f32[768]{0:T(1024)S(1)}, f32[768]{0:T(1024)S(1)}, f32[768]{0:T(1024)S(1)}, f32[768]{0:T(1024)S(1)}, f32[768]{0:T(1024)S(1)}, /*index=5*/f32[30...) all-reduce(f32[768]{0:T(1024)S(1)} %reduce_sum.291, ...), channel_id=5, replica_groups=mesh['items'=4,'rows'=8] {'items','rows'}, use_global_device_ids=true, to_apply=%region_30.31.clone | all-reduce | flops 9216 | bytes 73728
  992.5 27.5 %reduce-scatter.21.cloned.1.call-done = f32[24,768]{1,0:T(8,128)} async-done(((f32[768,768]{1,0:T(8,128)}), f32[24,768]{1,0:T(8,128)}) %reduce-scatter.21.cloned.1.call-update) | async-done | bytes 73744
  1020.0 104.5 %reduce-scatter.23.cloned.1.call-done = f32[24,768]{1,0:T(8,128)} async-done(((f32[768,768]{1,0:T(8,128)}), f32[24,768]{1,0:T(8,128)}) %reduce-scatter.23.cloned.1.call-update) | async-done | bytes 73744
  1124.5 141.6 %reduce-scatter.17.cloned.1.call-done = f32[96,768]{1,0:T(8,128)} async-done(((f32[3072,768]{1,0:T(8,128)}), f32[96,768]{1,0:T(8,128)}) %reduce-scatter.17.cloned.1.call-update) | async-done | bytes 294928 | tf_op jit(solution)/shard_map/reduce_scatter | solution.py:362
  1266.1 141.6 %reduce-scatter.15.cloned.1.call-done = f32[24,3072]{1,0:T(8,128)} async-done(((f32[768,3072]{1,0:T(8,128)}), f32[24,3072]{1,0:T(8,128)}) %reduce-scatter.15.cloned.1.call-update) | async-done | bytes 294928 | tf_op jit(solution)/shard_map/reduce_scatter | solution.py:360
  (438 shorter events, 507.0 us)
Async XLA Ops:
  7.2 63.6 %all-gather.8.cloned.1.call-start = ((), (), s32[]{:S(2)}) async-start(), calls=%async_computation.8 | async-start | bytes 1216512 | tf_op jit(solution)/shard_map/all_gather | solution.py:299
  7.9 153.3 %all-gather.6.cloned.1.call-start = ((), (), s32[]{:S(2)}) async-start(), calls=%async_computation.7 | async-start | bytes 1216512 | tf_op jit(solution)/shard_map/all_gather | solution.py:298
  8.7 246.9 %all-gather.10.cloned.1.call-start = ((), (), s32[]{:S(2)}) async-start(), calls=%async_computation.9 | async-start | bytes 1216512 | tf_op jit(solution)/shard_map/all_gather | solution.py:308
  9.4 272.9 %all-gather.12.cloned.1.call-start = ((), (), s32[]{:S(2)}) async-start(), calls=%async_computation.10 | async-start | bytes 4866048 | tf_op jit(solution)/shard_map/all_gather | solution.py:312
  11.8 61.3 %all-to-all-start = ((bf16[32,24,768]{2,1,0:T(8,128)(2,1)}), bf16[32,24,768]{2,1,0:T(8,128)(2,1)S(1)}, u32[]{:S(2)}, u32[]{:S(2)}) async-start(bf16[32,24,768]{2,1,0:T(8,128)(2,1)} %stack.17), calls=%async_computation | async-start | bytes 2359296 | tf_op jit(solution)/shard_map/all_to_all | solution.py:301
  19.2 327.8 %all-gather.14.cloned.1.call-start = ((), (), s32[]{:S(2)}) async-start(), calls=%async_computation.11 | async-start | bytes 4866048 | tf_op jit(solution)/shard_map/all_gather | solution.py:314
  76.1 90.5 %collective-permute-start = (bf16[2,512,768]{2,1,0:T(8,128)(2,1)}, bf16[2,512,768]{2,1,0:T(8,128)(2,1)}, u32[]{:S(2)}, u32[]{:S(2)}) collective-permute-start(bf16[2,512,768]{2,1,0:T(8,128)(2,1)} %pad_maximum_fusion.1), channel_id=1, source_target_pairs={{0,2},{1,3},{2,4},{3,5},{4,6},{5,7},{8,10},{9,11},{10,12},{11,13},... | collective-permute-start | bytes 4718600 | tf_op jit(solution)/shard_map/ppermute | solution.py:17
  79.6 88.5 %collective-permute-start.1 = (bf16[2,512,768]{2,1,0:T(8,128)(2,1)}, bf16[2,512,768]{2,1,0:T(8,128)(2,1)}, u32[]{:S(2)}, u32[]{:S(2)}) collective-permute-start(bf16[2,512,768]{2,1,0:T(8,128)(2,1)} %pad_maximum_fusion.1), channel_id=1, source_target_pairs={{0,1},{1,2},{2,3},{3,4},{4,5},{5,6},{6,7},{8,9},{9,10},{10,11},{11... | collective-permute-start | bytes 4718600 | tf_op jit(solution)/shard_map/ppermute | solution.py:17
  84.3 85.5 %collective-permute-start.2 = (bf16[2,512,768]{2,1,0:T(8,128)(2,1)}, bf16[2,512,768]{2,1,0:T(8,128)(2,1)}, u32[]{:S(2)}, u32[]{:S(2)}) collective-permute-start(bf16[2,512,768]{2,1,0:T(8,128)(2,1)} %pad_maximum_fusion.1), channel_id=1, source_target_pairs={{1,0},{2,1},{3,2},{4,3},{5,4},{6,5},{7,6},{9,8},{10,9},{11,10},{12... | collective-permute-start | bytes 4718600 | tf_op jit(solution)/shard_map/ppermute | solution.py:17
  85.6 85.7 %collective-permute-start.3 = (bf16[2,512,768]{2,1,0:T(8,128)(2,1)}, bf16[2,512,768]{2,1,0:T(8,128)(2,1)}, u32[]{:S(2)}, u32[]{:S(2)}) collective-permute-start(bf16[2,512,768]{2,1,0:T(8,128)(2,1)} %pad_maximum_fusion.1), channel_id=1, source_target_pairs={{2,0},{3,1},{4,2},{5,3},{6,4},{7,5},{10,8},{11,9},{12,10},{13,11},... | collective-permute-start | bytes 4718600 | tf_op jit(solution)/shard_map/ppermute | solution.py:17
  86.9 905.6 %reduce-scatter.13.cloned.1.call-start = ((), (), s32[]{:S(2)}) async-start(), calls=%async_computation.12 | async-start | bytes 2433024 | tf_op jit(solution)/shard_map/reduce_scatter | solution.py:356
  373.7 37.7 %collective-permute-start.4 = (bf16[2,512,768]{2,1,0:T(8,128)(2,1)}, bf16[2,512,768]{2,1,0:T(8,128)(2,1)}, u32[]{:S(2)}, u32[]{:S(2)}) collective-permute-start(bf16[2,512,768]{2,1,0:T(8,128)(2,1)} %pad_maximum_fusion.2), channel_id=1, source_target_pairs={{0,2},{1,3},{2,4},{3,5},{4,6},{5,7},{8,10},{9,11},{10,12},{11,13},... | collective-permute-start | bytes 4718600 | tf_op jit(solution)/shard_map/ppermute | solution.py:17
  378.2 71.2 %collective-permute-start.5 = (bf16[2,512,768]{2,1,0:T(8,128)(2,1)}, bf16[2,512,768]{2,1,0:T(8,128)(2,1)}, u32[]{:S(2)}, u32[]{:S(2)}) collective-permute-start(bf16[2,512,768]{2,1,0:T(8,128)(2,1)} %pad_maximum_fusion.2), channel_id=1, source_target_pairs={{0,1},{1,2},{2,3},{3,4},{4,5},{5,6},{6,7},{8,9},{9,10},{10,11},{11... | collective-permute-start | bytes 4718600 | tf_op jit(solution)/shard_map/ppermute | solution.py:17
  382.7 68.4 %collective-permute-start.6 = (bf16[2,512,768]{2,1,0:T(8,128)(2,1)}, bf16[2,512,768]{2,1,0:T(8,128)(2,1)}, u32[]{:S(2)}, u32[]{:S(2)}) collective-permute-start(bf16[2,512,768]{2,1,0:T(8,128)(2,1)} %pad_maximum_fusion.2), channel_id=1, source_target_pairs={{1,0},{2,1},{3,2},{4,3},{5,4},{6,5},{7,6},{9,8},{10,9},{11,10},{12... | collective-permute-start | bytes 4718600 | tf_op jit(solution)/shard_map/ppermute | solution.py:17
  384.0 69.2 %collective-permute-start.7 = (bf16[2,512,768]{2,1,0:T(8,128)(2,1)}, bf16[2,512,768]{2,1,0:T(8,128)(2,1)}, u32[]{:S(2)}, u32[]{:S(2)}) collective-permute-start(bf16[2,512,768]{2,1,0:T(8,128)(2,1)} %pad_maximum_fusion.2), channel_id=1, source_target_pairs={{2,0},{3,1},{4,2},{5,3},{6,4},{7,5},{10,8},{11,9},{12,10},{13,11},... | collective-permute-start | bytes 4718600 | tf_op jit(solution)/shard_map/ppermute | solution.py:17
  645.7 346.8 %reduce-scatter.19.cloned.1.call-start = ((), (), s32[]{:S(2)}) async-start(), calls=%async_computation.15 | async-start | bytes 2433024
  807.6 212.4 %reduce-scatter.21.cloned.1.call-start = ((), (), s32[]{:S(2)}) async-start(), calls=%async_computation.16 | async-start | bytes 2433024
  820.9 40.8 %collective-permute-start.10 = (bf16[2,512,768]{1,2,0:T(8,128)(2,1)S(1)}, bf16[2,512,768]{1,2,0:T(8,128)(2,1)S(1)}, u32[]{:S(2)}, u32[]{:S(2)}) collective-permute-start(bf16[2,512,768]{1,2,0:T(8,128)(2,1)S(1)} %get-tuple-element.505), channel_id=1, source_target_pairs={{0,1},{1,2},{2,3},{3,4},{4,5},{5,6},{6,7},{8,9},{9,10},{10,11},{11... | collective-permute-start | bytes 4718600 | tf_op jit(solution)/shard_map/ppermute | solution.py:17
  824.7 37.2 %collective-permute-start.11 = (bf16[2,512,768]{1,2,0:T(8,128)(2,1)S(1)}, bf16[2,512,768]{1,2,0:T(8,128)(2,1)S(1)}, u32[]{:S(2)}, u32[]{:S(2)}) collective-permute-start(bf16[2,512,768]{1,2,0:T(8,128)(2,1)S(1)} %get-tuple-element.504), channel_id=1, source_target_pairs={{0,2},{1,3},{2,4},{3,5},{4,6},{5,7},{8,10},{9,11},{10,12},{11,13},... | collective-permute-start | bytes 4718600 | tf_op jit(solution)/shard_map/ppermute | solution.py:17
  826.3 42.8 %collective-permute-start.8 = (bf16[2,512,768]{1,2,0:T(8,128)(2,1)S(1)}, bf16[2,512,768]{1,2,0:T(8,128)(2,1)S(1)}, u32[]{:S(2)}, u32[]{:S(2)}) collective-permute-start(bf16[2,512,768]{1,2,0:T(8,128)(2,1)S(1)} %get-tuple-element.503), channel_id=1, source_target_pairs={{2,0},{3,1},{4,2},{5,3},{6,4},{7,5},{10,8},{11,9},{12,10},{13,11},... | collective-permute-start | bytes 4718600 | tf_op jit(solution)/shard_map/ppermute | solution.py:17
  827.6 41.5 %collective-permute-start.9 = (bf16[2,512,768]{1,2,0:T(8,128)(2,1)S(1)}, bf16[2,512,768]{1,2,0:T(8,128)(2,1)S(1)}, u32[]{:S(2)}, u32[]{:S(2)}) collective-permute-start(bf16[2,512,768]{1,2,0:T(8,128)(2,1)S(1)} %get-tuple-element.506), channel_id=1, source_target_pairs={{1,0},{2,1},{3,2},{4,3},{5,4},{6,5},{7,6},{9,8},{10,9},{11,10},{12... | collective-permute-start | bytes 4718600 | tf_op jit(solution)/shard_map/ppermute | solution.py:17
  877.6 246.9 %reduce-scatter.23.cloned.1.call-start = ((), (), s32[]{:S(2)}) async-start(), calls=%async_computation.17 | async-start | bytes 2433024
  884.1 382.0 %reduce-scatter.17.cloned.1.call-start = ((), (), s32[]{:S(2)}) async-start(), calls=%async_computation.14 | async-start | bytes 9732096 | tf_op jit(solution)/shard_map/reduce_scatter | solution.py:362
  892.8 515.0 %reduce-scatter.15.cloned.1.call-start = ((), (), s32[]{:S(2)}) async-start(), calls=%async_computation.13 | async-start | bytes 9732096 | tf_op jit(solution)/shard_map/reduce_scatter | solution.py:360
  (41 other events, 504.7 us)
Sparse Core Ops, SparseCore 0:
  10.9 59.8 all-gather.7
  73.8 87.4 all-gather.5
  164.2 52.7 all-gather.9
  219.8 62.4 all-gather.11
  285.1 61.8 all-gather.13
  645.8 97.1 reduce-scatter.12
  807.8 107.6 reduce-scatter.18
  921.4 98.6 reduce-scatter.20
  1025.9 98.5 reduce-scatter.22
  1130.8 135.2 reduce-scatter.16
  1272.6 135.1 reduce-scatter.14
